TPU v7x, 32 devices: a whole 2x2x4 slice. The times are simulated.
32 devices in a mesh: agent: 8 (over y, x, core), res: 4 (over z).
Axes of the slice: x: 2, y: 2, z: 4, core: 2. Of those that a mesh axis runs over, the one named last changes fastest.
Arguments:
- linear_cost: float32 [2048, 2048], P('agent', 'res'), may hold values from -6 to 6
- agent_type: int32 [2048], P('agent'), may hold values from 0 to 3, as said below
- block_mask: int32 [2048, 16], P('agent', 'res'), may hold values 0 or 1
- inverses: bfloat16 [4, 2048, 2048], P(None, 'res'), as said below
- cost_weight: float32 [2048], P('res'), may hold values from 0.5 to 8
- target: float32 [2048], P('res'), may hold values from -6 to 6
Outputs:
- usage: float32 [2048, 2048], P('agent', 'res')
- shared: float32 [2048], P('res')
- prices: float32 [2048], P('res')
- primal_norm: float32 [5], replicated
- dual_norm: float32 [5], replicated
Inputs may be any that keep to these rules, and one draw needn't show every extreme that they name: Each inverses[k] is exactly symmetric: inverses[k, i, j] equals inverses[k, j, i]. `agent_type`: each aligned block of 256 agents (the agents held by one device along the agent axis) holds exactly 64 agents of each type, in no particular order.
All inputs are finite; a program needn't handle non-finite values. No bound on the sum of `block_mask` on one device may be relied on, other than what follows from the above.
Results may differ from a plain program's by a relative error of at most 0.0039.
Values may be sent and summed in bfloat16 or wider, within the bound.
No kernel may reach another device: no remote copies, remote signals or barrier semaphores. Data moves between devices by JAX's collectives and lax.ppermute only.
A program may use at most 64 MiB of HBM per device.

v0:
```python
import jax
import jax.numpy as jnp
from jax import lax
from jax.sharding import PartitionSpec as P

BLK = 128
ITERS = 5
penalty = 1.0
eps = 1e-06


def on_device(linear_cost, agent_type, block_mask, inverses, cost_weight, target):
    local_agents, local_width = linear_cost.shape
    type_count = inverses.shape[0]
    group_rows = local_agents // type_count
    count = local_agents * lax.axis_size("agent")
    block_count = block_mask.shape[1]
    order = jnp.argsort(agent_type, stable=True)
    restore = jnp.argsort(order, stable=True)
    expand = jnp.broadcast_to(
        block_mask.astype(jnp.float32)[:, :, None], (local_agents, block_count, BLK)
    ).reshape(local_agents, local_width)
    usage = jnp.zeros(linear_cost.shape, jnp.float32)
    mean_usage = jnp.zeros((local_width,), jnp.float32)
    shared = jnp.zeros((local_width,), jnp.float32)
    prices = jnp.zeros((local_width,), jnp.float32)
    primal_list = []
    dual_list = []
    for iteration in range(ITERS):
        rhs = (penalty * (usage - mean_usage + shared - prices) - linear_cost).astype(jnp.bfloat16)
        grouped = rhs[order].reshape(type_count, group_rows, local_width)
        product = jnp.einsum(
            "tas,tws->taw",
            lax.all_gather(grouped, "res", axis=2, tiled=True),
            inverses,
            preferred_element_type=jnp.float32,
        )
        new_usage = product.reshape(local_agents, local_width)[restore]
        new_usage = new_usage * expand
        change_local = penalty * penalty * jnp.sum((new_usage - usage) ** 2)
        usage = new_usage
        column_sum = jnp.sum(usage, axis=0)
        usage_sum = lax.psum(column_sum, "agent")
        dual2 = lax.psum(change_local, ("agent", "res"))
        mean_usage = usage_sum / count
        shared = (cost_weight * target + penalty * (prices + mean_usage)) / (cost_weight + penalty)
        prices = prices + mean_usage - shared
        primal2 = lax.psum(count * jnp.sum((mean_usage - shared) ** 2), "res")
        primal_list.append(jnp.sqrt(primal2 + eps))
        dual_list.append(jnp.sqrt(dual2 + eps))
    primal_norm = jnp.stack(primal_list)
    dual_norm = jnp.stack(dual_list)
    return (usage, shared, prices, primal_norm, dual_norm)


def solution(mesh):
    placed = (
        P("agent", "res"),
        P("agent"),
        P("agent", "res"),
        P(None, "res", None),
        P("res"),
        P("res"),
    )
    return jax.shard_map(
        on_device,
        mesh=mesh,
        in_specs=placed,
        out_specs=(P("agent", "res"), P("res"), P("res"), P(), P()),
        check_vma=False,
    )
```

profile of v0, /device:TPU:12, one launch (start us, length us, event | category | flops | bytes accessed | tf_op | source)
XLA Modules:
  0.0 334.9 jit_solution(6932095263842248031)
XLA Ops:
  7.2 3.8 %sort.31 = (s32[256]{0:T(256)}, s32[256]{0:T(256)S(1)}) sort(s32[256]{0:T(256)} %param.7, s32[256]{0:T(256)S(1)} %iota.7), dimensions={0}, to_apply=%region_0.0 | sort | flops 2048 | bytes 4096 | tf_op jit(solution)/shard_map/jit(argsort)/sort | solution.py:18
  11.1 1.1 subtract_convert_fusion.4
  12.2 1.9 gather_fusion
  14.1 3.2 sort.32
  18.2 25.1 %all-gather.6.cloned.1.call-done = bf16[4,64,2048]{2,1,0:T(8,128)(2,1)} async-done(((bf16[4,64,512]{2,1,0:T(8,128)(2,1)}), bf16[4,64,2048]{2,1,0:T(8,128)(2,1)}) %all-gather.6.cloned.1.call-update) | async-done | bytes 1048592 | tf_op jit(solution)/shard_map/all_gather | solution.py:34
  43.3 6.4 %fusion.13 = f32[4,64,512]{2,1,0:T(8,128)S(1)} fusion(bf16[4,64,2048]{2,1,0:T(8,128)(2,1)} %all-gather.6.cloned.1.call-done, bf16[4,512,2048]{2,1,0:T(8,128)(2,1)} %param.9), kind=kOutput, calls=%fused_computation.56 | convolution fusion | flops 536870912 | bytes 9961472 | tf_op jit(solution)/shard_map/tas,tws->taw/dot_general | solution.py:32
  49.7 1.0 gather_fusion.1
  51.1 11.9 %psum.105 = f32[512]{0:T(512)S(1)} all-reduce(f32[512]{0:T(512)S(1)} %get-tuple-element.44), channel_id=1, replica_groups=mesh['agent'=8,'res'=4] {'agent'}, use_global_device_ids=true, to_apply=%region_3.4 | all-reduce | flops 512 | bytes 4096 | tf_op jit(solution)/shard_map/psum | solution.py:43
  63.7 1.9 gather_fusion.2
  65.7 27.5 %all-gather.8.cloned.1.call-done = bf16[4,64,2048]{2,1,0:T(8,128)(2,1)} async-done(((bf16[4,64,512]{2,1,0:T(8,128)(2,1)}), bf16[4,64,2048]{2,1,0:T(8,128)(2,1)}) %all-gather.8.cloned.1.call-update) | async-done | bytes 1048592 | tf_op jit(solution)/shard_map/all_gather | solution.py:34
  93.1 6.4 %fusion.14 = f32[4,64,512]{2,1,0:T(8,128)S(1)} fusion(bf16[4,64,2048]{2,1,0:T(8,128)(2,1)} %all-gather.8.cloned.1.call-done, bf16[4,512,2048]{2,1,0:T(8,128)(2,1)} %param.9), kind=kOutput, calls=%fused_computation.57 | convolution fusion | flops 536870912 | bytes 9961472 | tf_op jit(solution)/shard_map/tas,tws->taw/dot_general | solution.py:32
  99.5 1.0 gather_fusion.3
  100.6 11.9 %psum.106 = f32[512]{0:T(512)S(1)} all-reduce(f32[512]{0:T(512)S(1)} %get-tuple-element.42), channel_id=1, replica_groups=mesh['agent'=8,'res'=4] {'agent'}, use_global_device_ids=true, to_apply=%region_5.6 | all-reduce | flops 512 | bytes 4096 | tf_op jit(solution)/shard_map/psum | solution.py:43
  113.2 1.9 gather_fusion.4
  115.1 27.5 %all-gather.10.cloned.1.call-done = bf16[4,64,2048]{2,1,0:T(8,128)(2,1)} async-done(((bf16[4,64,512]{2,1,0:T(8,128)(2,1)}), bf16[4,64,2048]{2,1,0:T(8,128)(2,1)}) %all-gather.10.cloned.1.call-update) | async-done | bytes 1048592 | tf_op jit(solution)/shard_map/all_gather | solution.py:34
  142.6 6.4 %fusion.15 = f32[4,64,512]{2,1,0:T(8,128)S(1)} fusion(bf16[4,64,2048]{2,1,0:T(8,128)(2,1)} %all-gather.10.cloned.1.call-done, bf16[4,512,2048]{2,1,0:T(8,128)(2,1)} %param.9), kind=kOutput, calls=%fused_computation.58 | convolution fusion | flops 536870912 | bytes 9961472 | tf_op jit(solution)/shard_map/tas,tws->taw/dot_general | solution.py:32
  148.9 1.0 gather_fusion.5
  150.0 12.1 %psum.107 = f32[512]{0:T(512)S(1)} all-reduce(f32[512]{0:T(512)S(1)} %get-tuple-element.40), channel_id=1, replica_groups=mesh['agent'=8,'res'=4] {'agent'}, use_global_device_ids=true, to_apply=%region_7.8 | all-reduce | flops 512 | bytes 4096 | tf_op jit(solution)/shard_map/psum | solution.py:43
  162.8 1.9 gather_fusion.6
  164.8 27.4 %all-gather.12.cloned.1.call-done = bf16[4,64,2048]{2,1,0:T(8,128)(2,1)} async-done(((bf16[4,64,512]{2,1,0:T(8,128)(2,1)}), bf16[4,64,2048]{2,1,0:T(8,128)(2,1)}) %all-gather.12.cloned.1.call-update) | async-done | bytes 1048592 | tf_op jit(solution)/shard_map/all_gather | solution.py:34
  192.2 6.4 %fusion.16 = f32[4,64,512]{2,1,0:T(8,128)S(1)} fusion(bf16[4,64,2048]{2,1,0:T(8,128)(2,1)} %all-gather.12.cloned.1.call-done, bf16[4,512,2048]{2,1,0:T(8,128)(2,1)} %param.9), kind=kOutput, calls=%fused_computation.59 | convolution fusion | flops 536870912 | bytes 9961472 | tf_op jit(solution)/shard_map/tas,tws->taw/dot_general | solution.py:32
  198.6 1.8 gather_fusion.7
  200.4 1.2 fusion.9
  201.5 11.9 %psum.108 = f32[512]{0:T(512)S(1)} all-reduce(f32[512]{0:T(512)S(1)} %get-tuple-element.38), channel_id=1, replica_groups=mesh['agent'=8,'res'=4] {'agent'}, use_global_device_ids=true, to_apply=%region_9.10 | all-reduce | flops 512 | bytes 4096 | tf_op jit(solution)/shard_map/psum | solution.py:43
  214.1 1.9 gather_fusion.8
  218.6 24.9 %all-gather.14.cloned.1.call-done = bf16[4,64,2048]{2,1,0:T(8,128)(2,1)} async-done(((bf16[4,64,512]{2,1,0:T(8,128)(2,1)}), bf16[4,64,2048]{2,1,0:T(8,128)(2,1)}) %all-gather.14.cloned.1.call-update) | async-done | bytes 1048592 | tf_op jit(solution)/shard_map/all_gather | solution.py:34
  243.5 6.4 %fusion.17 = f32[4,64,512]{2,1,0:T(8,128)S(1)} fusion(bf16[4,64,2048]{2,1,0:T(8,128)(2,1)} %all-gather.14.cloned.1.call-done, bf16[4,512,2048]{2,1,0:T(8,128)(2,1)} %param.9), kind=kOutput, calls=%fused_computation.60 | convolution fusion | flops 536870912 | bytes 9961472 | tf_op jit(solution)/shard_map/tas,tws->taw/dot_general | solution.py:32
  249.9 1.8 gather_fusion.9
  251.7 2.8 multiply_reduce_fusion
  254.5 11.9 %psum.109 = f32[512]{0:T(512)S(1)} all-reduce(f32[512]{0:T(512)S(1)} %get-tuple-element.14), channel_id=1, replica_groups=mesh['agent'=8,'res'=4] {'agent'}, use_global_device_ids=true, to_apply=%region_11.12 | all-reduce | flops 512 | bytes 4096 | tf_op jit(solution)/shard_map/psum | solution.py:43
  268.2 9.8 %all-reduce.1 = (f32[]{:T(128)}, f32[]{:T(128)}, f32[]{:T(128)}, f32[]{:T(128)}, f32[]{:T(128)}) all-reduce(f32[]{:T(128)S(6)} %mul.99, f32[]{:T(128)S(6)} %mul.100, f32[]{:T(128)S(6)} %mul.101, f32[]{:T(128)S(6)} %mul.102, f32[]{:T(128)S(6)} %mul.103), channel_id=1, replica_groups=mesh['agent'=8,'res'=4] {'res'}, use_global_device_ids=true, to_apply=%region_13.14 | all-reduce | flops 5 | bytes 40 | tf_op jit(solution)/shard_map/psum | solution.py:48
  281.3 42.5 %all-reduce = (f32[]{:T(128)}, f32[]{:T(128)}, f32[]{:T(128)}, f32[]{:T(128)}, f32[]{:T(128)}) all-reduce(f32[]{:T(128)} %get-tuple-element.13, f32[]{:T(128)} %get-tuple-element.12, f32[]{:T(128)} %get-tuple-element.11, f32[]{:T(128)} %get-tuple-element.10, f32[]{:T(128)} %get-tuple-element.9), channel_id=1, replica_groups=mesh['agent'=8,'res'=4] {'agent','res'}, use_global_device_ids=true, to_apply=%region_23.24 | all-reduce | flops 5 | bytes 40 | tf_op jit(solution)/shard_map/psum | solution.py:44
  (45 shorter events, 7.2 us)
Async XLA Ops:
  7.2 36.1 %all-gather.6.cloned.1.call-start = ((), (), s32[]{:S(2)}) async-start(), calls=%async_computation | async-start | bytes 1310720 | tf_op jit(solution)/shard_map/all_gather | solution.py:34
  14.0 79.1 %all-gather.8.cloned.1.call-start = ((), (), s32[]{:S(2)}) async-start(), calls=%async_computation.1 | async-start | bytes 1310720 | tf_op jit(solution)/shard_map/all_gather | solution.py:34
  18.1 44.9 %copy-start.1 = (f32[512]{0:T(512)S(1)}, f32[512]{0:T(512)}, u32[]{:S(2)}) copy-start(f32[512]{0:T(512)} %param.10) | copy-start | bytes 6148
  18.1 44.9 %copy-start.3 = (f32[512]{0:T(512)S(1)}, f32[512]{0:T(512)}, u32[]{:S(2)}) copy-start(f32[512]{0:T(512)} %param.11) | copy-start | bytes 6148
  18.1 45.5 %copy-start = (f32[256,512]{1,0:T(8,128)S(1)}, f32[256,512]{1,0:T(8,128)}, u32[]{:S(2)}) copy-start(f32[256,512]{1,0:T(8,128)} %param.6) | copy-start | bytes 1572868
  65.6 77.0 %all-gather.10.cloned.1.call-start = ((), (), s32[]{:S(2)}) async-start(), calls=%async_computation.2 | async-start | bytes 1310720 | tf_op jit(solution)/shard_map/all_gather | solution.py:34
  115.1 77.2 %all-gather.12.cloned.1.call-start = ((), (), s32[]{:S(2)}) async-start(), calls=%async_computation.3 | async-start | bytes 1310720 | tf_op jit(solution)/shard_map/all_gather | solution.py:34
  164.7 78.8 %all-gather.14.cloned.1.call-start = ((), (), s32[]{:S(2)}) async-start(), calls=%async_computation.4 | async-start | bytes 1310720 | tf_op jit(solution)/shard_map/all_gather | solution.py:34
  267.0 61.4 %copy-start.2 = (f32[512]{0:T(512)}, f32[512]{0:T(512)S(1)}, u32[]{:S(2)}) copy-start(f32[512]{0:T(512)S(1)} %get-tuple-element.26) | copy-start | bytes 6148
Sparse Core Ops, SparseCore 0:
  14.2 29.0 all-gather.5
  65.7 27.3 all-gather.7
  115.2 27.3 all-gather.9
  164.8 27.3 all-gather.11
  216.1 27.3 all-gather.13
where the time goes:
time: 336 us; the launch traced here: 335 us
  waiting for transfers between devices  132 us (39%)
  blocking collectives  112 us (33%)
  matrix products  31.9 us (9%)
  between operations  23.8 us (7%)
  local copies, waits for them, and re-layouts  17.4 us (5%)
  other arithmetic  17.3 us (5%)
    all_gather x5, waiting for transfers between devices, on_device(): lax.all_gather(grouped, 'res', axis=2, tiled=True)  132 us
    psum x5, blocking collectives, on_device(): usage_sum = lax.psum(column_sum, 'agent')  59.6 us
    psum x1, blocking collectives, on_device(): dual2 = lax.psum(change_local, ('agent', 'res'))  42.5 us
    dot_general x5, matrix products, on_device(): jnp.einsum('tas,tws->taw', lax.all_gather(grouped, 'res', axis=2, tiled=T...  31.9 us
    psum x1, blocking collectives, on_device(): primal2 = lax.psum(count * jnp.sum((mean_usage - shared) ** 2), 'res')  9.78 us
    gather x5, local copies, waits for them, and re-layouts, on_device(): grouped = rhs[order].reshape(type_count, group_rows, local_width)  9.27 us
  transfers between devices with their start and end apart: 5, of which 5 were waited for; matrix products, arithmetic and copies ran while one was open for 1% of the time, Pallas kernels for 0%

commit v1 on v0

--- a/solution.py
+++ b/solution.py
@@ -7,6 +7,18 @@
 ITERS = 5
 penalty = 1.0
 eps = 1e-06
+
+
+def product_in_turn(array, axis, dim, product):
+    length, here, rows = (lax.axis_size(axis), lax.axis_index(axis), array.shape[dim])
+    right = [(i, (i + 1) % length) for i in range(length)]
+    block, total = (array, None)
+    for step in range(length):
+        coming = lax.ppermute(block, axis, right) if step < length - 1 else None
+        update = product(block, (here - step) % length * rows)
+        total = update if total is None else total + update
+        block = coming
+    return total
 
 
 def on_device(linear_cost, agent_type, block_mask, inverses, cost_weight, target):
@@ -29,11 +41,16 @@
     for iteration in range(ITERS):
         rhs = (penalty * (usage - mean_usage + shared - prices) - linear_cost).astype(jnp.bfloat16)
         grouped = rhs[order].reshape(type_count, group_rows, local_width)
-        product = jnp.einsum(
-            "tas,tws->taw",
-            lax.all_gather(grouped, "res", axis=2, tiled=True),
-            inverses,
-            preferred_element_type=jnp.float32,
+        product = product_in_turn(
+            grouped,
+            "res",
+            2,
+            lambda part, offset: jnp.einsum(
+                "tas,tws->taw",
+                part,
+                lax.dynamic_slice_in_dim(inverses, offset, part.shape[2], axis=2),
+                preferred_element_type=jnp.float32,
+            ),
         )
         new_usage = product.reshape(local_agents, local_width)[restore]
         new_usage = new_usage * expand

time: 336 us -> 295 us (0.88); the launches traced: 335 us -> 290 us
  waiting for transfers between devices: 132 us -> 86.3 us
  matrix products: 31.9 us -> 47.1 us
  between operations: 23.8 us -> 10.8 us
  starting transfers between devices: 0.21 us -> 4.4 us
  local copies, waits for them, and re-layouts: 17.4 us -> 13.9 us
    all_gather x5 -> x0, waiting for transfers between devices: 132 us -> none  [on_device(): lax.all_gather(grouped, 'res', axis=2, tiled=True)]
    ppermute x0 -> x15, waiting for transfers between devices: none -> 86.3 us  [product_in_turn(): coming = lax.ppermute(block, axis, right) if step < length - 1 else None]
    dot_general x5 -> x20, matrix products: 31.9 us -> 47.1 us  [on_device(): jnp.einsum('tas,tws->taw', part, lax.dynamic_slice_in_dim(inverses, offse...]
    ppermute x0 -> x15, starting transfers between devices: none -> 4.4 us  [product_in_turn(): coming = lax.ppermute(block, axis, right) if step < length - 1 else None]
    gather x5, local copies, waits for them, and re-layouts: 9.27 us -> 5.77 us  [on_device(): grouped = rhs[order].reshape(type_count, group_rows, local_width)]
  transfers between devices with their start and end apart: 5 -> 15, of which waited for: 5 -> 15; matrix products, arithmetic and copies ran while one was open for 1% -> 14% of each run, Pallas kernels for 0% -> 0%
where the time goes in v1:
time: 295 us; the launch traced here: 290 us
  blocking collectives  111 us (38%)
  waiting for transfers between devices  86.3 us (29%)
  matrix products  47.1 us (16%)
  other arithmetic  17.3 us (6%)
  local copies, waits for them, and re-layouts  13.9 us (5%)
  between operations  10.8 us (4%)
  starting transfers between devices  4.4 us (1%)
    ppermute x15, waiting for transfers between devices, product_in_turn(): coming = lax.ppermute(block, axis, right) if step < length - 1 else None  86.3 us
    psum x5, blocking collectives, on_device(): usage_sum = lax.psum(column_sum, 'agent')  59 us
    dot_general x20, matrix products, on_device(): jnp.einsum('tas,tws->taw', part, lax.dynamic_slice_in_dim(inverses, offse...  47.1 us
    psum x1, blocking collectives, on_device(): dual2 = lax.psum(change_local, ('agent', 'res'))  43 us
    psum x1, blocking collectives, on_device(): primal2 = lax.psum(count * jnp.sum((mean_usage - shared) ** 2), 'res')  8.66 us
    gather x5, local copies, waits for them, and re-layouts, on_device(): new_usage = product.reshape(local_agents, local_width)[restore]  6.44 us
  transfers between devices with their start and end apart: 15, of which 15 were waited for; matrix products, arithmetic and copies ran while one was open for 14% of the time, Pallas kernels for 0%

profile of v1, /device:TPU:12, one launch (start us, length us, event | category | flops | bytes accessed | tf_op | source)
XLA Modules:
  0.0 290.5 jit_solution(1435112417140896543)
XLA Ops:
  0.6 3.8 %sort.31 = (s32[256]{0:T(256)}, s32[256]{0:T(256)S(1)}) sort(s32[256]{0:T(256)} %param.7, s32[256]{0:T(256)S(1)} %iota.7), dimensions={0}, to_apply=%region_0.0 | sort | flops 2048 | bytes 4096 | tf_op jit(solution)/shard_map/jit(argsort)/sort | solution.py:30
  8.4 3.2 %sort.32 = (s32[256]{0:T(256)}, s32[256]{0:T(256)S(1)}) sort(s32[256]{0:T(256)S(1)} %get-tuple-element.7, s32[256]{0:T(256)S(1)} %iota.8), dimensions={0}, to_apply=%region_1.2 | sort | flops 2048 | bytes 4096 | tf_op jit(solution)/shard_map/jit(argsort)/sort | solution.py:31
  11.5 3.3 %collective-permute-done = bf16[4,64,512]{2,1,0:T(8,128)(2,1)S(1)} collective-permute-done((bf16[4,64,512]{2,1,0:T(8,128)(2,1)S(1)}, bf16[4,64,512]{2,1,0:T(8,128)(2,1)S(1)}, u32[]{:S(2)}, u32[]{:S(2)}) %collective-permute-start) | collective-permute-done | bytes 262176 | tf_op jit(solution)/shard_map/ppermute | solution.py:17
  19.6 3.0 %collective-permute-done.1 = bf16[4,64,512]{2,1,0:T(8,128)(2,1)S(1)} collective-permute-done((bf16[4,64,512]{2,1,0:T(8,128)(2,1)S(1)}, bf16[4,64,512]{2,1,0:T(8,128)(2,1)S(1)}, u32[]{:S(2)}, u32[]{:S(2)}) %collective-permute-start.1) | collective-permute-done | bytes 262176 | tf_op jit(solution)/shard_map/ppermute | solution.py:17
  25.9 2.3 convolution_add_fusion.13
  28.3 2.6 collective-permute-done.2
  34.6 11.8 %psum.105 = f32[512]{0:T(512)S(1)} all-reduce(f32[512]{0:T(512)S(1)} %get-tuple-element.44), channel_id=1, replica_groups=mesh['agent'=8,'res'=4] {'agent'}, use_global_device_ids=true, to_apply=%region_3.4 | all-reduce | flops 512 | bytes 4096 | tf_op jit(solution)/shard_map/psum | solution.py:60
  48.4 9.8 %collective-permute-done.3 = bf16[4,64,512]{2,1,0:T(8,128)(2,1)S(1)} collective-permute-done((bf16[4,64,512]{2,1,0:T(8,128)(2,1)S(1)}, bf16[4,64,512]{2,1,0:T(8,128)(2,1)S(1)}, u32[]{:S(2)}, u32[]{:S(2)}) %collective-permute-start.3) | collective-permute-done | bytes 262176 | tf_op jit(solution)/shard_map/ppermute | solution.py:17
  60.6 6.6 %collective-permute-done.4 = bf16[4,64,512]{2,1,0:T(8,128)(2,1)S(1)} collective-permute-done((bf16[4,64,512]{2,1,0:T(8,128)(2,1)S(1)}, bf16[4,64,512]{2,1,0:T(8,128)(2,1)S(1)}, u32[]{:S(2)}, u32[]{:S(2)}) %collective-permute-start.4) | collective-permute-done | bytes 262176 | tf_op jit(solution)/shard_map/ppermute | solution.py:17
  69.6 2.3 convolution_add_fusion.10
  71.9 3.4 %collective-permute-done.5 = bf16[4,64,512]{2,1,0:T(8,128)(2,1)S(1)} collective-permute-done((bf16[4,64,512]{2,1,0:T(8,128)(2,1)S(1)}, bf16[4,64,512]{2,1,0:T(8,128)(2,1)S(1)}, u32[]{:S(2)}, u32[]{:S(2)}) %collective-permute-start.5) | collective-permute-done | bytes 262176 | tf_op jit(solution)/shard_map/ppermute | solution.py:17
  75.3 2.3 convolution_add_fusion.9
  78.8 11.8 %psum.106 = f32[512]{0:T(512)S(1)} all-reduce(f32[512]{0:T(512)S(1)} %get-tuple-element.42), channel_id=1, replica_groups=mesh['agent'=8,'res'=4] {'agent'}, use_global_device_ids=true, to_apply=%region_5.6 | all-reduce | flops 512 | bytes 4096 | tf_op jit(solution)/shard_map/psum | solution.py:60
  92.5 9.9 %collective-permute-done.6 = bf16[4,64,512]{2,1,0:T(8,128)(2,1)S(1)} collective-permute-done((bf16[4,64,512]{2,1,0:T(8,128)(2,1)S(1)}, bf16[4,64,512]{2,1,0:T(8,128)(2,1)S(1)}, u32[]{:S(2)}, u32[]{:S(2)}) %collective-permute-start.6) | collective-permute-done | bytes 262176 | tf_op jit(solution)/shard_map/ppermute | solution.py:17
  104.8 6.7 %collective-permute-done.7 = bf16[4,64,512]{2,1,0:T(8,128)(2,1)S(1)} collective-permute-done((bf16[4,64,512]{2,1,0:T(8,128)(2,1)S(1)}, bf16[4,64,512]{2,1,0:T(8,128)(2,1)S(1)}, u32[]{:S(2)}, u32[]{:S(2)}) %collective-permute-start.7) | collective-permute-done | bytes 262176 | tf_op jit(solution)/shard_map/ppermute | solution.py:17
  113.8 2.3 convolution_add_fusion.7
  116.1 3.5 %collective-permute-done.8 = bf16[4,64,512]{2,1,0:T(8,128)(2,1)S(1)} collective-permute-done((bf16[4,64,512]{2,1,0:T(8,128)(2,1)S(1)}, bf16[4,64,512]{2,1,0:T(8,128)(2,1)S(1)}, u32[]{:S(2)}, u32[]{:S(2)}) %collective-permute-start.8) | collective-permute-done | bytes 262176 | tf_op jit(solution)/shard_map/ppermute | solution.py:17
  123.0 11.8 %psum.107 = f32[512]{0:T(512)S(1)} all-reduce(f32[512]{0:T(512)S(1)} %get-tuple-element.40), channel_id=1, replica_groups=mesh['agent'=8,'res'=4] {'agent'}, use_global_device_ids=true, to_apply=%region_7.8 | all-reduce | flops 512 | bytes 4096 | tf_op jit(solution)/shard_map/psum | solution.py:60
  136.8 9.9 %collective-permute-done.9 = bf16[4,64,512]{2,1,0:T(8,128)(2,1)S(1)} collective-permute-done((bf16[4,64,512]{2,1,0:T(8,128)(2,1)S(1)}, bf16[4,64,512]{2,1,0:T(8,128)(2,1)S(1)}, u32[]{:S(2)}, u32[]{:S(2)}) %collective-permute-start.9) | collective-permute-done | bytes 262176 | tf_op jit(solution)/shard_map/ppermute | solution.py:17
  149.0 6.7 %collective-permute-done.10 = bf16[4,64,512]{2,1,0:T(8,128)(2,1)S(1)} collective-permute-done((bf16[4,64,512]{2,1,0:T(8,128)(2,1)S(1)}, bf16[4,64,512]{2,1,0:T(8,128)(2,1)S(1)}, u32[]{:S(2)}, u32[]{:S(2)}) %collective-permute-start.10) | collective-permute-done | bytes 262176 | tf_op jit(solution)/shard_map/ppermute | solution.py:17
  158.0 2.4 convolution_add_fusion.4
  160.4 3.5 %collective-permute-done.11 = bf16[4,64,512]{2,1,0:T(8,128)(2,1)S(1)} collective-permute-done((bf16[4,64,512]{2,1,0:T(8,128)(2,1)S(1)}, bf16[4,64,512]{2,1,0:T(8,128)(2,1)S(1)}, u32[]{:S(2)}, u32[]{:S(2)}) %collective-permute-start.11) | collective-permute-done | bytes 262176 | tf_op jit(solution)/shard_map/ppermute | solution.py:17
  169.1 11.8 %psum.108 = f32[512]{0:T(512)S(1)} all-reduce(f32[512]{0:T(512)S(1)} %get-tuple-element.38), channel_id=1, replica_groups=mesh['agent'=8,'res'=4] {'agent'}, use_global_device_ids=true, to_apply=%region_9.10 | all-reduce | flops 512 | bytes 4096 | tf_op jit(solution)/shard_map/psum | solution.py:60
  182.9 9.9 %collective-permute-done.12 = bf16[4,64,512]{2,1,0:T(8,128)(2,1)S(1)} collective-permute-done((bf16[4,64,512]{2,1,0:T(8,128)(2,1)S(1)}, bf16[4,64,512]{2,1,0:T(8,128)(2,1)S(1)}, u32[]{:S(2)}, u32[]{:S(2)}) %collective-permute-start.12) | collective-permute-done | bytes 262176 | tf_op jit(solution)/shard_map/ppermute | solution.py:17
  195.4 2.4 fusion.15
  197.8 4.1 %collective-permute-done.13 = bf16[4,64,512]{2,1,0:T(8,128)(2,1)} collective-permute-done((bf16[4,64,512]{2,1,0:T(8,128)(2,1)S(1)}, bf16[4,64,512]{2,1,0:T(8,128)(2,1)}, u32[]{:S(2)}, u32[]{:S(2)}) %collective-permute-start.13) | collective-permute-done | bytes 262176 | tf_op jit(solution)/shard_map/ppermute | solution.py:17
  204.2 2.5 convolution_add_fusion.1
  206.7 3.6 %collective-permute-done.14 = bf16[4,64,512]{2,1,0:T(8,128)(2,1)S(1)} collective-permute-done((bf16[4,64,512]{2,1,0:T(8,128)(2,1)}, bf16[4,64,512]{2,1,0:T(8,128)(2,1)S(1)}, u32[]{:S(2)}, u32[]{:S(2)}) %collective-permute-start.14) | collective-permute-done | bytes 262176 | tf_op jit(solution)/shard_map/ppermute | solution.py:17
  214.3 2.8 multiply_reduce_fusion
  217.2 43.0 %all-reduce = (f32[]{:T(128)}, f32[]{:T(128)}, f32[]{:T(128)}, f32[]{:T(128)}, f32[]{:T(128)}) all-reduce(f32[]{:T(128)} %get-tuple-element.13, f32[]{:T(128)} %get-tuple-element.12, f32[]{:T(128)} %get-tuple-element.11, f32[]{:T(128)} %get-tuple-element.10, f32[]{:T(128)} %get-tuple-element.9), channel_id=1, replica_groups=mesh['agent'=8,'res'=4] {'agent','res'}, use_global_device_ids=true, to_apply=%region_23.24 | all-reduce | flops 5 | bytes 40 | tf_op jit(solution)/shard_map/psum | solution.py:61
  263.5 11.8 %psum.109 = f32[512]{0:T(512)S(1)} all-reduce(f32[512]{0:T(512)S(1)} %get-tuple-element.14), channel_id=1, replica_groups=mesh['agent'=8,'res'=4] {'agent'}, use_global_device_ids=true, to_apply=%region_11.12 | all-reduce | flops 512 | bytes 4096 | tf_op jit(solution)/shard_map/psum | solution.py:60
  276.6 8.7 %all-reduce.1 = (f32[]{:T(128)}, f32[]{:T(128)}, f32[]{:T(128)}, f32[]{:T(128)}, f32[]{:T(128)}) all-reduce(f32[]{:T(128)S(6)} %mul.131, f32[]{:T(128)S(6)} %mul.132, f32[]{:T(128)S(6)} %mul.133, f32[]{:T(128)S(6)} %mul.134, f32[]{:T(128)S(6)} %mul.135), channel_id=1, replica_groups=mesh['agent'=8,'res'=4] {'res'}, use_global_device_ids=true, to_apply=%region_13.14 | all-reduce | flops 5 | bytes 40 | tf_op jit(solution)/shard_map/psum | solution.py:65
  (77 shorter events, 56.2 us)
Async XLA Ops:
  6.7 8.1 %collective-permute-start = (bf16[4,64,512]{2,1,0:T(8,128)(2,1)S(1)}, bf16[4,64,512]{2,1,0:T(8,128)(2,1)S(1)}, u32[]{:S(2)}, u32[]{:S(2)}) collective-permute-start(bf16[4,64,512]{2,1,0:T(8,128)(2,1)S(1)} %bitcast.62), channel_id=1, source_target_pairs={{0,1},{1,2},{2,3},{3,0},{4,5},{5,6},{6,7},{7,4},{8,9},{9,10},{10,1... | collective-permute-start | bytes 786440 | tf_op jit(solution)/shard_map/ppermute | solution.py:17
  14.8 7.8 %collective-permute-start.1 = (bf16[4,64,512]{2,1,0:T(8,128)(2,1)S(1)}, bf16[4,64,512]{2,1,0:T(8,128)(2,1)S(1)}, u32[]{:S(2)}, u32[]{:S(2)}) collective-permute-start(bf16[4,64,512]{2,1,0:T(8,128)(2,1)S(1)} %collective-permute-done), channel_id=1, source_target_pairs={{0,1},{1,2},{2,3},{3,0},{4,5},{5,6},{6,7},{7,4},{8,9},{9,10},{10,1... | collective-permute-start | bytes 786440 | tf_op jit(solution)/shard_map/ppermute | solution.py:17
  19.6 26.8 %copy-start.2 = (f32[512]{0:T(512)S(1)}, f32[512]{0:T(512)}, u32[]{:S(2)}) copy-start(f32[512]{0:T(512)} %param.10) | copy-start | bytes 6148
  19.6 26.8 %copy-start.4 = (f32[512]{0:T(512)S(1)}, f32[512]{0:T(512)}, u32[]{:S(2)}) copy-start(f32[512]{0:T(512)} %param.11) | copy-start | bytes 6148
  19.6 27.4 %copy-start = (f32[256,512]{1,0:T(8,128)S(1)}, f32[256,512]{1,0:T(8,128)}, u32[]{:S(2)}) copy-start(f32[256,512]{1,0:T(8,128)} %param.6) | copy-start | bytes 1572868
  22.6 8.2 %collective-permute-start.2 = (bf16[4,64,512]{2,1,0:T(8,128)(2,1)S(1)}, bf16[4,64,512]{2,1,0:T(8,128)(2,1)S(1)}, u32[]{:S(2)}, u32[]{:S(2)}) collective-permute-start(bf16[4,64,512]{2,1,0:T(8,128)(2,1)S(1)} %collective-permute-done.1), channel_id=1, source_target_pairs={{0,1},{1,2},{2,3},{3,0},{4,5},{5,6},{6,7},{7,4},{8,9},{9,10},{10,1... | collective-permute-start | bytes 786440 | tf_op jit(solution)/shard_map/ppermute | solution.py:17
  48.3 9.9 %collective-permute-start.3 = (bf16[4,64,512]{2,1,0:T(8,128)(2,1)S(1)}, bf16[4,64,512]{2,1,0:T(8,128)(2,1)S(1)}, u32[]{:S(2)}, u32[]{:S(2)}) collective-permute-start(bf16[4,64,512]{2,1,0:T(8,128)(2,1)S(1)} %bitcast.66), channel_id=1, source_target_pairs={{0,1},{1,2},{2,3},{3,0},{4,5},{5,6},{6,7},{7,4},{8,9},{9,10},{10,1... | collective-permute-start | bytes 786440 | tf_op jit(solution)/shard_map/ppermute | solution.py:17
  58.2 9.0 %collective-permute-start.4 = (bf16[4,64,512]{2,1,0:T(8,128)(2,1)S(1)}, bf16[4,64,512]{2,1,0:T(8,128)(2,1)S(1)}, u32[]{:S(2)}, u32[]{:S(2)}) collective-permute-start(bf16[4,64,512]{2,1,0:T(8,128)(2,1)S(1)} %collective-permute-done.3), channel_id=1, source_target_pairs={{0,1},{1,2},{2,3},{3,0},{4,5},{5,6},{6,7},{7,4},{8,9},{9,10},{10,1... | collective-permute-start | bytes 786440 | tf_op jit(solution)/shard_map/ppermute | solution.py:17
  67.2 8.1 %collective-permute-start.5 = (bf16[4,64,512]{2,1,0:T(8,128)(2,1)S(1)}, bf16[4,64,512]{2,1,0:T(8,128)(2,1)S(1)}, u32[]{:S(2)}, u32[]{:S(2)}) collective-permute-start(bf16[4,64,512]{2,1,0:T(8,128)(2,1)S(1)} %collective-permute-done.4), channel_id=1, source_target_pairs={{0,1},{1,2},{2,3},{3,0},{4,5},{5,6},{6,7},{7,4},{8,9},{9,10},{10,1... | collective-permute-start | bytes 786440 | tf_op jit(solution)/shard_map/ppermute | solution.py:17
  92.5 10.0 %collective-permute-start.6 = (bf16[4,64,512]{2,1,0:T(8,128)(2,1)S(1)}, bf16[4,64,512]{2,1,0:T(8,128)(2,1)S(1)}, u32[]{:S(2)}, u32[]{:S(2)}) collective-permute-start(bf16[4,64,512]{2,1,0:T(8,128)(2,1)S(1)} %bitcast.68), channel_id=1, source_target_pairs={{0,1},{1,2},{2,3},{3,0},{4,5},{5,6},{6,7},{7,4},{8,9},{9,10},{10,1... | collective-permute-start | bytes 786440 | tf_op jit(solution)/shard_map/ppermute | solution.py:17
  102.4 9.0 %collective-permute-start.7 = (bf16[4,64,512]{2,1,0:T(8,128)(2,1)S(1)}, bf16[4,64,512]{2,1,0:T(8,128)(2,1)S(1)}, u32[]{:S(2)}, u32[]{:S(2)}) collective-permute-start(bf16[4,64,512]{2,1,0:T(8,128)(2,1)S(1)} %collective-permute-done.6), channel_id=1, source_target_pairs={{0,1},{1,2},{2,3},{3,0},{4,5},{5,6},{6,7},{7,4},{8,9},{9,10},{10,1... | collective-permute-start | bytes 786440 | tf_op jit(solution)/shard_map/ppermute | solution.py:17
  111.4 8.2 %collective-permute-start.8 = (bf16[4,64,512]{2,1,0:T(8,128)(2,1)S(1)}, bf16[4,64,512]{2,1,0:T(8,128)(2,1)S(1)}, u32[]{:S(2)}, u32[]{:S(2)}) collective-permute-start(bf16[4,64,512]{2,1,0:T(8,128)(2,1)S(1)} %collective-permute-done.7), channel_id=1, source_target_pairs={{0,1},{1,2},{2,3},{3,0},{4,5},{5,6},{6,7},{7,4},{8,9},{9,10},{10,1... | collective-permute-start | bytes 786440 | tf_op jit(solution)/shard_map/ppermute | solution.py:17
  136.7 9.9 %collective-permute-start.9 = (bf16[4,64,512]{2,1,0:T(8,128)(2,1)S(1)}, bf16[4,64,512]{2,1,0:T(8,128)(2,1)S(1)}, u32[]{:S(2)}, u32[]{:S(2)}) collective-permute-start(bf16[4,64,512]{2,1,0:T(8,128)(2,1)S(1)} %bitcast.70), channel_id=1, source_target_pairs={{0,1},{1,2},{2,3},{3,0},{4,5},{5,6},{6,7},{7,4},{8,9},{9,10},{10,1... | collective-permute-start | bytes 786440 | tf_op jit(solution)/shard_map/ppermute | solution.py:17
  146.7 9.0 %collective-permute-start.10 = (bf16[4,64,512]{2,1,0:T(8,128)(2,1)S(1)}, bf16[4,64,512]{2,1,0:T(8,128)(2,1)S(1)}, u32[]{:S(2)}, u32[]{:S(2)}) collective-permute-start(bf16[4,64,512]{2,1,0:T(8,128)(2,1)S(1)} %collective-permute-done.9), channel_id=1, source_target_pairs={{0,1},{1,2},{2,3},{3,0},{4,5},{5,6},{6,7},{7,4},{8,9},{9,10},{10,1... | collective-permute-start | bytes 786440 | tf_op jit(solution)/shard_map/ppermute | solution.py:17
  155.7 8.2 %collective-permute-start.11 = (bf16[4,64,512]{2,1,0:T(8,128)(2,1)S(1)}, bf16[4,64,512]{2,1,0:T(8,128)(2,1)S(1)}, u32[]{:S(2)}, u32[]{:S(2)}) collective-permute-start(bf16[4,64,512]{2,1,0:T(8,128)(2,1)S(1)} %collective-permute-done.10), channel_id=1, source_target_pairs={{0,1},{1,2},{2,3},{3,0},{4,5},{5,6},{6,7},{7,4},{8,9},{9,10},{10,1... | collective-permute-start | bytes 786440 | tf_op jit(solution)/shard_map/ppermute | solution.py:17
  182.8 11.9 %copy-start.1 = (bf16[256,512]{1,0:T(8,128)(2,1)}, bf16[256,512]{1,0:T(8,128)(2,1)S(1)}, u32[]{:S(2)}) copy-start(bf16[256,512]{1,0:T(8,128)(2,1)S(1)} %gather_fusion.8) | copy-start | bytes 786436
  182.8 9.9 %collective-permute-start.12 = (bf16[4,64,512]{2,1,0:T(8,128)(2,1)S(1)}, bf16[4,64,512]{2,1,0:T(8,128)(2,1)S(1)}, u32[]{:S(2)}, u32[]{:S(2)}) collective-permute-start(bf16[4,64,512]{2,1,0:T(8,128)(2,1)S(1)} %bitcast.64), channel_id=1, source_target_pairs={{0,1},{1,2},{2,3},{3,0},{4,5},{5,6},{6,7},{7,4},{8,9},{9,10},{10,1... | collective-permute-start | bytes 786440 | tf_op jit(solution)/shard_map/ppermute | solution.py:17
  192.7 9.1 %collective-permute-start.13 = (bf16[4,64,512]{2,1,0:T(8,128)(2,1)S(1)}, bf16[4,64,512]{2,1,0:T(8,128)(2,1)}, u32[]{:S(2)}, u32[]{:S(2)}) collective-permute-start(bf16[4,64,512]{2,1,0:T(8,128)(2,1)S(1)} %collective-permute-done.12), channel_id=1, source_target_pairs={{0,1},{1,2},{2,3},{3,0},{4,5},{5,6},{6,7},{7,4},{8,9},{9,10},{10,1... | collective-permute-start | bytes 786440 | tf_op jit(solution)/shard_map/ppermute | solution.py:17
  201.9 8.4 %collective-permute-start.14 = (bf16[4,64,512]{2,1,0:T(8,128)(2,1)}, bf16[4,64,512]{2,1,0:T(8,128)(2,1)S(1)}, u32[]{:S(2)}, u32[]{:S(2)}) collective-permute-start(bf16[4,64,512]{2,1,0:T(8,128)(2,1)} %collective-permute-done.13), channel_id=1, source_target_pairs={{0,1},{1,2},{2,3},{3,0},{4,5},{5,6},{6,7},{7,4},{8,9},{9,10},{10,1... | collective-permute-start | bytes 786440 | tf_op jit(solution)/shard_map/ppermute | solution.py:17
  275.9 14.5 %copy-start.3 = (f32[512]{0:T(512)}, f32[512]{0:T(512)S(1)}, u32[]{:S(2)}) copy-start(f32[512]{0:T(512)S(1)} %get-tuple-element.26) | copy-start | bytes 6148
